TPU v7x, 32 devices: a whole 2x2x4 slice. The times are simulated.
32 devices in a mesh: section: 2 (over core), ep: 4 (over z), tp: 4 (over y, x).
Axes of the slice: x: 2, y: 2, z: 4, core: 2. Of those that a mesh axis runs over, the one named last changes fastest.
Arguments:
- hidden: bfloat16 [512, 6144], P('ep', ('section', 'tp')), may hold values from -6 to 6
- expert_ids: int32 [512, 2], P('ep'), may hold values from 0 to 7, all different within a row; in each aligned block of 128 rows (0 to 127, 128 to 255, ...) at most 40 rows name the same one
- gate_weights: float32 [512, 2], P('ep'), may hold values from 0 to 1, as said below
- gate_proj: bfloat16 [4, 6144, 16384], P('ep', None, ('section', 'tp')), may hold values from -0.078125 to 0.078125
- up_proj: bfloat16 [4, 6144, 16384], P('ep', None, ('section', 'tp')), may hold values from -0.078125 to 0.078125
- down_proj: bfloat16 [4, 6144, 16384], P('ep', ('section', 'tp')), may hold values from -0.0625 to 0.0625
Outputs:
- moe_out: bfloat16 [512, 6144], P('ep', ('section', 'tp'))
Inputs may be any that keep to these rules, and one draw needn't show every extreme that they name: `expert_ids`: the two entries of a row differ. Within the 128 rows of one device no expert is named by more than 40 rows, and in some device's rows one expert is named by exactly 40. Every expert is named somewhere. `gate_weights`: the two weights of a token are positive, sum to one, and the first is at least the second.
All inputs are finite; a program needn't handle non-finite values.
Results may differ from a plain program's by a relative error of at most 0.0059.
Values may be sent and summed in bfloat16 or wider, within the bound.
A program may use at most 192 MiB of HBM per device.

v0:
```python
import jax
import jax.numpy as jnp
from jax import lax
from jax.experimental import pallas as pl
from jax.experimental.pallas import tpu as pltpu
from jax.sharding import PartitionSpec as P

E = 8
F = 8192
CAP = 40


def slot_tables(expert_ids, capacity, experts):
    token_count = expert_ids.shape[0]
    flat_ids = expert_ids.reshape(-1)
    onehot = (flat_ids[:, None] == jnp.arange(experts, dtype=jnp.int32)[None, :]).astype(jnp.int32)
    before = jnp.cumsum(onehot, axis=0) - onehot
    position = jnp.sum(before * onehot, axis=1)
    slot_of = (flat_ids * capacity + position).reshape(token_count, -1)
    slot_range = jnp.arange(experts * capacity, dtype=jnp.int32)
    matches_st = slot_of[None, :, :] == slot_range[:, None, None]
    dispatch = jnp.any(matches_st, axis=2).astype(jnp.bfloat16)
    return (dispatch, slot_of)


def on_device(hidden, expert_ids, gate_weights, gate_proj, up_proj, down_proj):
    ep_count = lax.axis_size("ep")
    share_count = lax.axis_size("section") * lax.axis_size("tp")
    owners_each = max(1, ep_count // E)
    experts_each = max(1, E // ep_count)
    local_cols = gate_proj.shape[2]
    group_cols = local_cols * share_count
    owner_index = lax.axis_index("ep")
    share_index = lax.axis_index("section") * lax.axis_size("tp") + lax.axis_index("tp")
    own_expert = (owner_index * group_cols + share_index * local_cols) // F
    slot_expert = owner_index // owners_each * experts_each + jnp.arange(
        experts_each, dtype=jnp.int32
    )
    keep_mask = (slot_expert == own_expert).reshape(1, experts_each, 1, 1)
    gate_local = gate_proj[0]
    up_local = up_proj[0]
    down_local = down_proj[0]
    dispatch, slot_of = slot_tables(expert_ids, CAP, E)
    packed = jnp.dot(
        dispatch,
        lax.all_gather(hidden, ("section", "tp"), axis=1, tiled=True),
        preferred_element_type=jnp.float32,
    ).astype(jnp.bfloat16)
    grouped = packed.reshape(E // experts_each, experts_each, CAP, packed.shape[1])
    received = lax.all_to_all(
        jnp.repeat(grouped, owners_each, axis=0), "ep", split_axis=0, concat_axis=0, tiled=True
    )
    flat_rows = received.reshape(-1, received.shape[3])
    gate_out = jnp.dot(flat_rows, gate_local, preferred_element_type=jnp.float32)
    up_out = jnp.dot(flat_rows, up_local, preferred_element_type=jnp.float32)
    lead_shape = received.shape[:3]
    activated = (jax.nn.silu(gate_out) * up_out).reshape(lead_shape + (local_cols,))
    activated = jnp.where(keep_mask, activated, 0.0).astype(jnp.bfloat16)
    flat_act = activated.reshape(-1, local_cols)
    outputs = lax.dot_general(
        lax.all_gather(flat_act, ("section", "tp"), axis=1, tiled=True),
        down_local,
        (((1,), (1,)), ((), ())),
        preferred_element_type=jnp.float32,
    )
    outputs = outputs.reshape(lead_shape + (down_local.shape[0],)).astype(jnp.bfloat16)
    returned = lax.all_to_all(outputs, "ep", split_axis=0, concat_axis=0, tiled=True)
    grouped = returned.astype(jnp.float32).reshape(
        E // experts_each, owners_each, experts_each, CAP, returned.shape[3]
    )
    summed = jnp.sum(grouped, axis=1).reshape(E * CAP, returned.shape[3])
    first_rows = summed[slot_of[:, 0]]
    second_rows = summed[slot_of[:, 1]]
    combined_out = gate_weights[:, 0:1] * first_rows + gate_weights[:, 1:2] * second_rows
    return combined_out.astype(jnp.bfloat16)

SLOTS = 10
PARTS = 3
CHUNKS = 4
MESH = pl.DeviceIdType.MESH


def layer_kernel(
    hidden_ref, dispatch_ref, picks_ref, weights_ref, gate_ref, up_ref, down_ref, out_ref,
    sent, landed, across, x_all, w_buf, d_buf, acc, act_all, totals, back, ret,
    z_send, z_recv, s_send, s_recv, x_send, x_recv, a_send, a_recv, c_send, c_recv, r_send, r_recv, w_sem, d_sem,
):
    width = hidden_ref.shape[1]
    part = width // PARTS
    rows = 4 * CAP
    half = rows // 2
    units = 2 * PARTS
    cols = gate_ref.shape[2]
    chunk = cols // CHUNKS
    steps = 4 * units
    section = lax.axis_index("section")
    z = lax.axis_index("ep")
    tp = lax.axis_index("tp")
    tx, ty = tp % 2, tp // 2
    other = 1 - section

    def place(rel):
        return (ty + rel // 2) % 2 * 2 + (tx + rel % 2) % 2

    x_near, y_near, far = place(1), place(2), place(3)

    def weight_copies(step):
        rel, unit = step // units, step % units
        core = (section + unit % 2) % 2
        row = pl.multiple_of(((core * 4 + place(rel)) * PARTS + unit // 2) * part, part)
        slot = step % SLOTS
        return [
            pltpu.make_async_copy(ref.at[0, pl.ds(row, part), :], w_buf.at[slot, i], w_sem.at[slot, i])
            for i, ref in enumerate((gate_ref, up_ref))
        ]

    def down_copy(index):
        at = pl.multiple_of(index * chunk, chunk)
        return pltpu.make_async_copy(down_ref.at[0, :, pl.ds(at, chunk)], d_buf.at[index], d_sem.at[index])

    @pl.loop(0, SLOTS)
    def _(step):
        for copy in weight_copies(step):
            copy.start()

    @pl.loop(0, 8 * CHUNKS)
    def _(index):
        down_copy(index).start()

    barrier = pltpu.get_barrier_semaphore()
    for d in range(1, 4):
        pl.semaphore_signal(barrier, inc=1, device_id={"ep": (z + d) % 4}, device_id_type=MESH)
    pl.semaphore_signal(barrier, inc=1, device_id={"section": other}, device_id_type=MESH)
    pl.semaphore_signal(barrier, inc=1, device_id={"tp": x_near}, device_id_type=MESH)
    pl.semaphore_signal(barrier, inc=1, device_id={"tp": y_near}, device_id_type=MESH)

    packed = jnp.dot(dispatch_ref[...], hidden_ref[...], preferred_element_type=jnp.float32)
    packed = packed.astype(jnp.bfloat16)
    for g in range(4):
        for h in range(PARTS):
            sent[g, h] = packed[g * 2 * CAP : (g + 1) * 2 * CAP, h * part : (h + 1) * part]
    pl.semaphore_wait(barrier, 6)

    def remote(src, dst, send, recv, target):
        return pltpu.make_async_remote_copy(
            src_ref=src, dst_ref=dst, send_sem=send, recv_sem=recv, device_id=target, device_id_type=MESH
        )

    def z_copy(h, d):
        g = (z + d) % 4
        return remote(sent.at[g, h], landed.at[z, h], z_send.at[h, g], z_recv.at[h, z], {"ep": g})

    def z_arrival(h, d):
        g = (z + d) % 4
        return remote(sent.at[g, h], landed.at[g, h], z_send.at[h, g], z_recv.at[h, g], {"ep": g})

    @pl.loop(0, PARTS)
    def _(h):
        for d in (2, 1, 3):
            z_copy(h, d).start()

    for h in range(PARTS):
        landed[z, h] = sent[z, h]
    acc[...] = jnp.zeros_like(acc)
    totals[...] = jnp.zeros_like(totals)

    def spread(buf, at, send, recv, kind, unit):
        if kind < 2:
            index, target = at(tp, unit), {"tp": (x_near, y_near)[kind]}
            ref = buf.at[index]
        else:
            index, target = at((x_near, y_near)[kind - 2], unit), {"tp": (y_near, x_near)[kind - 2]}
            ref = buf.at[index, pl.ds((half, 0)[kind - 2], half), :]
        return remote(ref, ref, send.at[kind, unit], recv.at[kind, unit], target)

    def arrival(buf, at, send, recv, kind, unit):
        if kind < 2:
            ref = buf.at[at((x_near, y_near)[kind], unit)]
        else:
            ref = buf.at[at(far, unit), pl.ds((half, 0)[kind - 2], half), :]
        return remote(ref, ref, send.at[kind, unit], recv.at[kind, unit], {"tp": (x_near, y_near, y_near, x_near)[kind]})

    def x_at(place_of, unit):
        return place_of * units + unit

    x_args = (x_all, x_at, x_send, x_recv)

    def swap_copy(h):
        return remote(
            across.at[h], x_all.at[x_at(tp, 2 * h + 1)], s_send.at[h], s_recv.at[h], {"section": other}
        )

    @pl.loop(0, PARTS)
    def _(h):
        for d in (1, 3, 2):
            z_arrival(h, d).wait_recv()
        blocks = [landed[g, h].astype(jnp.float32) for g in range(4)]
        first = jnp.concatenate([b[:CAP] for b in blocks], axis=0)
        second = jnp.concatenate([b[CAP:] for b in blocks], axis=0)
        across[h] = jnp.where(section == 0, second, first).astype(jnp.bfloat16)
        swap_copy(h).start()
        x_all[x_at(tp, 2 * h)] = jnp.where(section == 0, first, second).astype(jnp.bfloat16)
        spread(*x_args, 0, 2 * h).start()
        spread(*x_args, 1, 2 * h).start()
        swap_copy(h).wait_recv()
        spread(*x_args, 0, 2 * h + 1).start()
        spread(*x_args, 1, 2 * h + 1).start()

    def gate_step(rel, unit):
        step = rel * units + unit
        slot = step % SLOTS
        for copy in weight_copies(step):
            copy.wait()
        x = x_all[x_at(place(rel), unit)]
        for i in range(2):
            for j in range(CHUNKS):
                acc[i, j] += jnp.dot(
                    x, w_buf[slot, i, :, j * chunk : (j + 1) * chunk], preferred_element_type=jnp.float32
                )

        @pl.when(step + SLOTS < steps)
        def _():
            for copy in weight_copies(step + SLOTS):
                copy.start()

    @pl.loop(0, units)
    def _(unit):
        gate_step(0, unit)
        for kind in range(2):
            arrival(*x_args, kind, unit).wait_recv()
            spread(*x_args, kind + 2, unit).start()

    @pl.loop(0, 2 * units)
    def _(k):
        gate_step(1 + k // units, k % units)

    @pl.loop(0, units)
    def _(unit):
        for kind in (2, 3):
            arrival(*x_args, kind, unit).wait_recv()
        gate_step(3, unit)

    def act_at(place_of, j, core=None):
        return ((section if core is None else core) * 4 + place_of) * CHUNKS + j

    a_args = (act_all, act_at, a_send, a_recv)

    def cross_copy(rel, j):
        ref = act_all.at[act_at(place(rel), j)]
        return remote(ref, ref, c_send.at[rel, j], c_recv.at[rel, j], {"section": other})

    def cross_arrival(rel, j):
        ref = act_all.at[act_at(place(rel), j, other)]
        return remote(ref, ref, c_send.at[rel, j], c_recv.at[rel, j], {"section": other})

    def down_step(core, rel, j):
        index = act_at(place(rel), j, core)
        down_copy(index).wait()
        totals[core] += lax.dot_general(
            act_all[index], d_buf[index], (((1,), (1,)), ((), ())), preferred_element_type=jnp.float32
        )

    @pl.loop(0, CHUNKS)
    def _(j):
        gate_out = acc[0, j]
        act_all[act_at(tp, j)] = (gate_out / (1.0 + jnp.exp(-gate_out)) * acc[1, j]).astype(jnp.bfloat16)
        spread(*a_args, 0, j).start()
        spread(*a_args, 1, j).start()
        cross_copy(0, j).start()

    @pl.loop(0, CHUNKS)
    def _(j):
        down_step(section, 0, j)
        cross_arrival(0, j).wait_recv()
        down_step(other, 0, j)
        for kind in range(2):
            arrival(*a_args, kind, j).wait_recv()
            spread(*a_args, kind + 2, j).start()
            cross_copy(kind + 1, j).start()

    @pl.loop(0, CHUNKS)
    def _(j):
        down_step(section, 1, j)
        down_step(section, 2, j)
        for kind in (2, 3):
            arrival(*a_args, kind, j).wait_recv()
        cross_copy(3, j).start()
        for rel in (1, 2):
            cross_arrival(rel, j).wait_recv()
            down_step(other, rel, j)
        down_step(section, 3, j)

    @pl.loop(0, CHUNKS)
    def _(j):
        cross_arrival(3, j).wait_recv()
        down_step(other, 3, j)

    def back_copy(d):
        g = (z + d) % 4
        return remote(back.at[g], ret.at[z], r_send.at[g], r_recv.at[z], {"ep": g})

    def back_arrival(d):
        g = (z + d) % 4
        return remote(back.at[g], ret.at[g], r_send.at[g], r_recv.at[g], {"ep": g})

    for g in range(4):
        back[g] = jnp.concatenate(
            [totals[e, g * CAP : (g + 1) * CAP, :] for e in range(2)], axis=0
        ).astype(jnp.bfloat16)
    for d in (2, 1, 3):
        back_copy(d).start()
    ret[z] = back[z]
    for d in (1, 3, 2):
        back_arrival(d).wait_recv()
    both = jnp.dot(
        picks_ref[...], ret[...].reshape(8 * CAP, width), preferred_element_type=jnp.float32
    )
    tokens = hidden_ref.shape[0]
    combined = weights_ref[:, 0:1] * both[:tokens] + weights_ref[:, 1:2] * both[tokens:]
    out_ref[...] = combined.astype(out_ref.dtype)

    for d in range(1, 4):
        back_copy(d).wait_send()

    @pl.loop(0, PARTS)
    def _(h):
        for d in range(1, 4):
            z_copy(h, d).wait_send()
        swap_copy(h).wait_send()

    @pl.loop(0, units)
    def _(unit):
        for kind in range(4):
            spread(*x_args, kind, unit).wait_send()

    @pl.loop(0, CHUNKS)
    def _(j):
        for kind in range(4):
            spread(*a_args, kind, j).wait_send()
        for rel in range(4):
            cross_copy(rel, j).wait_send()


def on_device_paired(hidden, expert_ids, gate_weights, gate_proj, up_proj, down_proj):
    tokens, width = hidden.shape
    cols = gate_proj.shape[2]
    part, chunk, rows = width // PARTS, cols // CHUNKS, 4 * CAP
    dispatch, slot_of = slot_tables(expert_ids, CAP, E)
    slot_range = jnp.arange(E * CAP, dtype=jnp.int32)[None, :]
    picks = (slot_of.T.reshape(-1, 1) == slot_range).astype(jnp.bfloat16)
    vmem = pl.BlockSpec(memory_space=pltpu.VMEM)
    anywhere = pl.BlockSpec(memory_space=pl.ANY)
    sem = pltpu.SemaphoreType.DMA
    return pl.pallas_call(
        layer_kernel,
        out_shape=jax.ShapeDtypeStruct((tokens, width), jnp.bfloat16),
        in_specs=[vmem] * 4 + [anywhere] * 3,
        out_specs=vmem,
        scratch_shapes=[
            pltpu.VMEM((4, PARTS, 2 * CAP, part), jnp.bfloat16),
            pltpu.VMEM((4, PARTS, 2 * CAP, part), jnp.bfloat16),
            pltpu.VMEM((PARTS, rows, part), jnp.bfloat16),
            pltpu.VMEM((8 * PARTS, rows, part), jnp.bfloat16),
            pltpu.VMEM((SLOTS, 2, part, cols), jnp.bfloat16),
            pltpu.VMEM((8 * CHUNKS, width, chunk), jnp.bfloat16),
            pltpu.VMEM((2, CHUNKS, rows, chunk), jnp.float32),
            pltpu.VMEM((8 * CHUNKS, rows, chunk), jnp.bfloat16),
            pltpu.VMEM((2, rows, width), jnp.float32),
            pltpu.VMEM((4, 2 * CAP, width), jnp.bfloat16),
            pltpu.VMEM((4, 2 * CAP, width), jnp.bfloat16),
            sem((PARTS, 4)), sem((PARTS, 4)), sem((PARTS,)), sem((PARTS,)),
            sem((4, 2 * PARTS)), sem((4, 2 * PARTS)), sem((4, CHUNKS)), sem((4, CHUNKS)),
            sem((4, CHUNKS)), sem((4, CHUNKS)), sem((4,)), sem((4,)),
            sem((SLOTS, 2)), sem((8 * CHUNKS,)),
        ],
        compiler_params=pltpu.CompilerParams(
            collective_id=0, has_side_effects=True, vmem_limit_bytes=62 * 1024 * 1024
        ),
    )(hidden, dispatch, picks, gate_weights, gate_proj, up_proj, down_proj)


def solution(mesh):
    def body(*args):
        paired = mesh.shape["ep"] == 4 and mesh.shape["section"] == 2 and mesh.shape["tp"] == 4
        paired = paired and E // mesh.shape["ep"] == mesh.shape["section"] and args[3].shape[2] * mesh.shape["tp"] == F
        return (on_device_paired if paired else on_device)(*args)

    return jax.shard_map(
        body,
        mesh=mesh,
        in_specs=(
            P("ep", ("section", "tp")),
            P("ep", None),
            P("ep", None),
            P("ep", None, ("section", "tp")),
            P("ep", None, ("section", "tp")),
            P("ep", ("section", "tp"), None),
        ),
        out_specs=P("ep", ("section", "tp")),
        check_vma=False,
    )
```

profile of v0, /device:TPU:0, one launch (start us, length us, event | category | flops | bytes accessed | tf_op | source)
XLA Modules:
  0.0 84.1 jit_solution(9127296832301096884)
XLA Ops:
  0.0 0.8 copy.27
  0.8 0.1 eq.57
  0.9 0.1 eq.53
  1.1 0.6 reduce-window.6
  1.7 0.2 slice_reduce_fusion
  1.9 0.1 fusion.3
  2.0 0.1 reduce_sum.12
  2.2 0.1 copy.29
  2.2 0.7 multiply_add_fusion
  3.0 0.7 convert_element_type.15.dispatch_ref
  3.6 1.4 %copy.30.weights_ref = f32[128,2]{1,0:T(8,128)} copy(f32[128,2]{0,1:T(2,128)} %param.8) | data formatting | bytes 2048 | tf_op args[2]
  5.0 0.8 fusion.picks_ref
  5.8 76.7 %shard_map.64 = bf16[128,768]{1,0:T(8,128)(2,1)} custom-call(bf16[128,768]{1,0:T(8,128)(2,1)} %hidden_ref.1, bf16[320,128]{1,0:T(8,128)(2,1)} %convert_element_type.15.dispatch_ref, bf16[256,320]{1,0:T(8,128)(2,1)} %fusion.picks_ref, f32[128,2]{1,0:T(8,128)} %copy.30.weights_ref, bf16[1,6144,2048]{2,1,0:T(8,128)(2,1)} %gate_ref.1, ...), custom_call_target="tpu_custom_call" | custom-call | tf_op jit(solution)/shard_map/pallas_call | solution.py:354
  82.5 1.6 %copy.32 = bf16[128,768]{1,0:T(8,128)(2,1)} copy(bf16[128,768]{1,0:T(8,128)(2,1)} %shard_map.64) | data formatting | bytes 393216
  (4 shorter events, 0.1 us)
where the time goes:
time: 84.6 us; the launch traced here: 84.1 us
  Pallas kernels  76.7 us (91%)
  local copies, waits for them, and re-layouts  4.5 us (5%)
  other arithmetic  2.9 us (3%)
    pallas_call x1, Pallas kernels, on_device_paired(): pl.pallas_call(layer_kernel, out_shape=jax.ShapeDtypeStruct((tokens, widt...  76.7 us
    unnamed x3, local copies, waits for them, and re-layouts  3.81 us

commit v1 on v0

--- a/solution.py
+++ b/solution.py
@@ -81,14 +81,16 @@
 
 
 def layer_kernel(
-    hidden_ref, dispatch_ref, picks_ref, weights_ref, gate_ref, up_ref, down_ref, out_ref,
-    sent, landed, across, x_all, w_buf, d_buf, acc, act_all, totals, back, ret,
+    hidden_ref, ids_ref, weights_ref, gate_ref, up_ref, down_ref, out_ref,
+    picks, scales, sent, landed, across, x_all, w_buf, d_buf, acc, act_all, totals, back, ret,
     z_send, z_recv, s_send, s_recv, x_send, x_recv, a_send, a_recv, c_send, c_recv, r_send, r_recv, w_sem, d_sem,
 ):
     width = hidden_ref.shape[1]
     part = width // PARTS
     rows = 4 * CAP
     half = rows // 2
+    tokens = hidden_ref.shape[0]
+    order = (0, 3, 1, 2)
     units = 2 * PARTS
     cols = gate_ref.shape[2]
     chunk = cols // CHUNKS
@@ -118,15 +120,6 @@
         at = pl.multiple_of(index * chunk, chunk)
         return pltpu.make_async_copy(down_ref.at[0, :, pl.ds(at, chunk)], d_buf.at[index], d_sem.at[index])
 
-    @pl.loop(0, SLOTS)
-    def _(step):
-        for copy in weight_copies(step):
-            copy.start()
-
-    @pl.loop(0, 8 * CHUNKS)
-    def _(index):
-        down_copy(index).start()
-
     barrier = pltpu.get_barrier_semaphore()
     for d in range(1, 4):
         pl.semaphore_signal(barrier, inc=1, device_id={"ep": (z + d) % 4}, device_id_type=MESH)
@@ -134,7 +127,29 @@
     pl.semaphore_signal(barrier, inc=1, device_id={"tp": x_near}, device_id_type=MESH)
     pl.semaphore_signal(barrier, inc=1, device_id={"tp": y_near}, device_id_type=MESH)
 
-    packed = jnp.dot(dispatch_ref[...], hidden_ref[...], preferred_element_type=jnp.float32)
+    @pl.loop(0, SLOTS)
+    def _(step):
+        for copy in weight_copies(step):
+            copy.start()
+
+    experts = lax.broadcasted_iota(jnp.int32, (2 * E, tokens), 0)
+    hot = [experts == ids_ref[k : k + 1, :] for k in range(2)]
+    named = jnp.where(hot[0] | hot[1], 1.0, 0.0).astype(jnp.bfloat16)
+    ahead = lax.broadcasted_iota(jnp.int32, (tokens, tokens), 0) < lax.broadcasted_iota(
+        jnp.int32, (tokens, tokens), 1
+    )
+    earlier = jnp.dot(
+        named, jnp.where(ahead, 1.0, 0.0).astype(jnp.bfloat16), preferred_element_type=jnp.float32
+    )
+    slots = lax.broadcasted_iota(jnp.int32, (E * CAP, tokens), 0).astype(jnp.float32)
+    chosen = []
+    for k in range(2):
+        position = jnp.sum(jnp.where(hot[k], earlier, 0.0), axis=0, keepdims=True)
+        slot = ids_ref[k : k + 1, :].astype(jnp.float32) * CAP + position
+        chosen.append(jnp.where(slots == slot, 1.0, 0.0))
+        picks[k] = chosen[k].astype(jnp.bfloat16)
+    dispatch = (chosen[0] + chosen[1]).astype(jnp.bfloat16)
+    packed = jnp.dot(dispatch, hidden_ref[...], preferred_element_type=jnp.float32)
     packed = packed.astype(jnp.bfloat16)
     for g in range(4):
         for h in range(PARTS):
@@ -159,10 +174,21 @@
         for d in (2, 1, 3):
             z_copy(h, d).start()
 
+    @pl.loop(0, 8 * CHUNKS)
+    def _(index):
+        down_copy(index).start()
+
     for h in range(PARTS):
         landed[z, h] = sent[z, h]
+    for k in range(2):
+        scales[k] = jnp.broadcast_to(weights_ref[k : k + 1, :], (tokens, tokens)).T
     acc[...] = jnp.zeros_like(acc)
     totals[...] = jnp.zeros_like(totals)
+
+    def part_of(buf, index, kind):
+        if buf is x_all:
+            return buf.at[index, pl.ds((half, 0)[kind - 2], half), :]
+        return buf.at[index, :, pl.ds((chunk // 2, 0)[kind - 2], chunk // 2)]
 
     def spread(buf, at, send, recv, kind, unit):
         if kind < 2:
@@ -170,14 +196,14 @@
             ref = buf.at[index]
         else:
             index, target = at((x_near, y_near)[kind - 2], unit), {"tp": (y_near, x_near)[kind - 2]}
-            ref = buf.at[index, pl.ds((half, 0)[kind - 2], half), :]
+            ref = part_of(buf, index, kind)
         return remote(ref, ref, send.at[kind, unit], recv.at[kind, unit], target)
 
     def arrival(buf, at, send, recv, kind, unit):
         if kind < 2:
             ref = buf.at[at((x_near, y_near)[kind], unit)]
         else:
-            ref = buf.at[at(far, unit), pl.ds((half, 0)[kind - 2], half), :]
+            ref = part_of(buf, at(far, unit), kind)
         return remote(ref, ref, send.at[kind, unit], recv.at[kind, unit], {"tp": (x_near, y_near, y_near, x_near)[kind]})
 
     def x_at(place_of, unit):
@@ -189,22 +215,6 @@
         return remote(
             across.at[h], x_all.at[x_at(tp, 2 * h + 1)], s_send.at[h], s_recv.at[h], {"section": other}
         )
-
-    @pl.loop(0, PARTS)
-    def _(h):
-        for d in (1, 3, 2):
-            z_arrival(h, d).wait_recv()
-        blocks = [landed[g, h].astype(jnp.float32) for g in range(4)]
-        first = jnp.concatenate([b[:CAP] for b in blocks], axis=0)
-        second = jnp.concatenate([b[CAP:] for b in blocks], axis=0)
-        across[h] = jnp.where(section == 0, second, first).astype(jnp.bfloat16)
-        swap_copy(h).start()
-        x_all[x_at(tp, 2 * h)] = jnp.where(section == 0, first, second).astype(jnp.bfloat16)
-        spread(*x_args, 0, 2 * h).start()
-        spread(*x_args, 1, 2 * h).start()
-        swap_copy(h).wait_recv()
-        spread(*x_args, 0, 2 * h + 1).start()
-        spread(*x_args, 1, 2 * h + 1).start()
 
     def gate_step(rel, unit):
         step = rel * units + unit
@@ -223,16 +233,34 @@
             for copy in weight_copies(step + SLOTS):
                 copy.start()
 
+    @pl.loop(0, PARTS)
+    def _(h):
+        for d in (1, 3, 2):
+            z_arrival(h, d).wait_recv()
+        blocks = [landed[g, h].astype(jnp.float32) for g in order]
+        first = jnp.concatenate([b[:CAP] for b in blocks], axis=0)
+        second = jnp.concatenate([b[CAP:] for b in blocks], axis=0)
+        across[h] = jnp.where(section == 0, second, first).astype(jnp.bfloat16)
+        swap_copy(h).start()
+        x_all[x_at(tp, 2 * h)] = jnp.where(section == 0, first, second).astype(jnp.bfloat16)
+        spread(*x_args, 0, 2 * h).start()
+        spread(*x_args, 1, 2 * h).start()
+        swap_copy(h).wait_recv()
+        spread(*x_args, 0, 2 * h + 1).start()
+        spread(*x_args, 1, 2 * h + 1).start()
+        gate_step(0, 2 * h)
+        gate_step(0, 2 * h + 1)
+
     @pl.loop(0, units)
     def _(unit):
-        gate_step(0, unit)
         for kind in range(2):
             arrival(*x_args, kind, unit).wait_recv()
             spread(*x_args, kind + 2, unit).start()
-
-    @pl.loop(0, 2 * units)
-    def _(k):
-        gate_step(1 + k // units, k % units)
+        gate_step(1, unit)
+
+    @pl.loop(0, units)
+    def _(unit):
+        gate_step(2, unit)
 
     @pl.loop(0, units)
     def _(unit):
@@ -240,87 +268,135 @@
             arrival(*x_args, kind, unit).wait_recv()
         gate_step(3, unit)
 
-    def act_at(place_of, j, core=None):
-        return ((section if core is None else core) * 4 + place_of) * CHUNKS + j
+    def act_at(place_of, unit, core=None):
+        return ((section if core is None else core) * 4 + place_of) * 2 * CHUNKS + unit
 
     a_args = (act_all, act_at, a_send, a_recv)
 
-    def cross_copy(rel, j):
-        ref = act_all.at[act_at(place(rel), j)]
-        return remote(ref, ref, c_send.at[rel, j], c_recv.at[rel, j], {"section": other})
-
-    def cross_arrival(rel, j):
-        ref = act_all.at[act_at(place(rel), j, other)]
-        return remote(ref, ref, c_send.at[rel, j], c_recv.at[rel, j], {"section": other})
-
-    def down_step(core, rel, j):
-        index = act_at(place(rel), j, core)
-        down_copy(index).wait()
-        totals[core] += lax.dot_general(
-            act_all[index], d_buf[index], (((1,), (1,)), ((), ())), preferred_element_type=jnp.float32
+    def cross_copy(rel, unit):
+        ref = act_all.at[act_at(place(rel), unit)]
+        return remote(ref, ref, c_send.at[rel, unit], c_recv.at[rel, unit], {"section": other})
+
+    def cross_arrival(rel, unit):
+        ref = act_all.at[act_at(place(rel), unit, other)]
+        return remote(ref, ref, c_send.at[rel, unit], c_recv.at[rel, unit], {"section": other})
+
+    def down_step(core, rel, r, j):
+        index = (core * 4 + place(rel)) * CHUNKS + j
+        if r == 0:
+            down_copy(index).wait()
+        totals[core, r] += lax.dot_general(
+            act_all[act_at(place(rel), r * CHUNKS + j, core)], d_buf[index], (((1,), (1,)), ((), ())),
+            preferred_element_type=jnp.float32,
         )
 
-    @pl.loop(0, CHUNKS)
-    def _(j):
-        gate_out = acc[0, j]
-        act_all[act_at(tp, j)] = (gate_out / (1.0 + jnp.exp(-gate_out)) * acc[1, j]).astype(jnp.bfloat16)
-        spread(*a_args, 0, j).start()
-        spread(*a_args, 1, j).start()
-        cross_copy(0, j).start()
-
-    @pl.loop(0, CHUNKS)
-    def _(j):
-        down_step(section, 0, j)
-        cross_arrival(0, j).wait_recv()
-        down_step(other, 0, j)
+    def activate(r, j):
+        unit = r * CHUNKS + j
+        gate_out = acc[0, j, r * half : (r + 1) * half]
+        up_out = acc[1, j, r * half : (r + 1) * half]
+        act_all[act_at(tp, unit)] = (gate_out / (1.0 + jnp.exp(-gate_out)) * up_out).astype(jnp.bfloat16)
+        spread(*a_args, 0, unit).start()
+        spread(*a_args, 1, unit).start()
+        cross_copy(0, unit).start()
+
+    def pass_on(unit):
         for kind in range(2):
-            arrival(*a_args, kind, j).wait_recv()
-            spread(*a_args, kind + 2, j).start()
-            cross_copy(kind + 1, j).start()
-
-    @pl.loop(0, CHUNKS)
-    def _(j):
-        down_step(section, 1, j)
-        down_step(section, 2, j)
+            arrival(*a_args, kind, unit).wait_recv()
+            spread(*a_args, kind + 2, unit).start()
+            cross_copy(kind + 1, unit).start()
+
+    def far_in(unit):
         for kind in (2, 3):
-            arrival(*a_args, kind, j).wait_recv()
-        cross_copy(3, j).start()
+            arrival(*a_args, kind, unit).wait_recv()
+        cross_copy(3, unit).start()
+
+    def own_steps(r, j):
+        down_step(section, 0, r, j)
+        cross_arrival(0, r * CHUNKS + j).wait_recv()
+        down_step(other, 0, r, j)
+
+    def rest_steps(r, j):
         for rel in (1, 2):
-            cross_arrival(rel, j).wait_recv()
-            down_step(other, rel, j)
-        down_step(section, 3, j)
-
-    @pl.loop(0, CHUNKS)
-    def _(j):
-        cross_arrival(3, j).wait_recv()
-        down_step(other, 3, j)
-
-    def back_copy(d):
-        g = (z + d) % 4
+            cross_arrival(rel, r * CHUNKS + j).wait_recv()
+            down_step(other, rel, r, j)
+        down_step(section, 3, r, j)
+
+    def last_steps(r, j):
+        cross_arrival(3, r * CHUNKS + j).wait_recv()
+        down_step(other, 3, r, j)
+
+    def back_copy(g):
         return remote(back.at[g], ret.at[z], r_send.at[g], r_recv.at[z], {"ep": g})
 
     def back_arrival(d):
         g = (z + d) % 4
         return remote(back.at[g], ret.at[g], r_send.at[g], r_recv.at[g], {"ep": g})
 
-    for g in range(4):
-        back[g] = jnp.concatenate(
-            [totals[e, g * CAP : (g + 1) * CAP, :] for e in range(2)], axis=0
-        ).astype(jnp.bfloat16)
-    for d in (2, 1, 3):
-        back_copy(d).start()
-    ret[z] = back[z]
+    def give_back(r):
+        for i in range(2):
+            g = order[2 * r + i]
+            back[g] = jnp.concatenate(
+                [totals[e, r, i * CAP : (i + 1) * CAP, :] for e in range(2)], axis=0
+            ).astype(jnp.bfloat16)
+
+            @pl.when(z != g)
+            def _():
+                back_copy(g).start()
+
+            @pl.when(z == g)
+            def _():
+                ret[z] = back[g]
+
+    @pl.loop(0, CHUNKS)
+    def _(j):
+        activate(0, j)
+
+    @pl.loop(0, CHUNKS)
+    def _(j):
+        own_steps(0, j)
+        pass_on(j)
+        activate(1, j)
+
+    @pl.loop(0, CHUNKS)
+    def _(j):
+        down_step(section, 1, 0, j)
+        down_step(section, 2, 0, j)
+        far_in(j)
+        pass_on(CHUNKS + j)
+        rest_steps(0, j)
+
+    @pl.loop(0, CHUNKS)
+    def _(j):
+        last_steps(0, j)
+
+    give_back(0)
+
+    @pl.loop(0, CHUNKS)
+    def _(j):
+        own_steps(1, j)
+        down_step(section, 1, 1, j)
+        down_step(section, 2, 1, j)
+        far_in(CHUNKS + j)
+        rest_steps(1, j)
+
+    @pl.loop(0, CHUNKS)
+    def _(j):
+        last_steps(1, j)
+
+    give_back(1)
     for d in (1, 3, 2):
         back_arrival(d).wait_recv()
-    both = jnp.dot(
-        picks_ref[...], ret[...].reshape(8 * CAP, width), preferred_element_type=jnp.float32
-    )
-    tokens = hidden_ref.shape[0]
-    combined = weights_ref[:, 0:1] * both[:tokens] + weights_ref[:, 1:2] * both[tokens:]
+    flat = ret[...].reshape(8 * CAP, width)
+    combined = 0.0
+    for k in range(2):
+        taken = lax.dot_general(picks[k], flat, (((0,), (0,)), ((), ())), preferred_element_type=jnp.float32)
+        combined = combined + scales[k][:, 0:1] * taken
     out_ref[...] = combined.astype(out_ref.dtype)
 
-    for d in range(1, 4):
-        back_copy(d).wait_send()
+    for g in range(4):
+        @pl.when(z != g)
+        def _():
+            back_copy(g).wait_send()
 
     @pl.loop(0, PARTS)
     def _(h):
@@ -333,7 +409,7 @@
         for kind in range(4):
             spread(*x_args, kind, unit).wait_send()
 
-    @pl.loop(0, CHUNKS)
+    @pl.loop(0, 2 * CHUNKS)
     def _(j):
         for kind in range(4):
             spread(*a_args, kind, j).wait_send()
@@ -345,18 +421,17 @@
     tokens, width = hidden.shape
     cols = gate_proj.shape[2]
     part, chunk, rows = width // PARTS, cols // CHUNKS, 4 * CAP
-    dispatch, slot_of = slot_tables(expert_ids, CAP, E)
-    slot_range = jnp.arange(E * CAP, dtype=jnp.int32)[None, :]
-    picks = (slot_of.T.reshape(-1, 1) == slot_range).astype(jnp.bfloat16)
     vmem = pl.BlockSpec(memory_space=pltpu.VMEM)
     anywhere = pl.BlockSpec(memory_space=pl.ANY)
     sem = pltpu.SemaphoreType.DMA
     return pl.pallas_call(
         layer_kernel,
         out_shape=jax.ShapeDtypeStruct((tokens, width), jnp.bfloat16),
-        in_specs=[vmem] * 4 + [anywhere] * 3,
+        in_specs=[vmem] * 3 + [anywhere] * 3,
         out_specs=vmem,
         scratch_shapes=[
+            pltpu.VMEM((2, E * CAP, tokens), jnp.bfloat16),
+            pltpu.VMEM((2, tokens, tokens), jnp.float32),
             pltpu.VMEM((4, PARTS, 2 * CAP, part), jnp.bfloat16),
             pltpu.VMEM((4, PARTS, 2 * CAP, part), jnp.bfloat16),
             pltpu.VMEM((PARTS, rows, part), jnp.bfloat16),
@@ -364,19 +439,19 @@
             pltpu.VMEM((SLOTS, 2, part, cols), jnp.bfloat16),
             pltpu.VMEM((8 * CHUNKS, width, chunk), jnp.bfloat16),
             pltpu.VMEM((2, CHUNKS, rows, chunk), jnp.float32),
-            pltpu.VMEM((8 * CHUNKS, rows, chunk), jnp.bfloat16),
-            pltpu.VMEM((2, rows, width), jnp.float32),
+            pltpu.VMEM((16 * CHUNKS, rows // 2, chunk), jnp.bfloat16),
+            pltpu.VMEM((2, 2, rows // 2, width), jnp.float32),
             pltpu.VMEM((4, 2 * CAP, width), jnp.bfloat16),
             pltpu.VMEM((4, 2 * CAP, width), jnp.bfloat16),
             sem((PARTS, 4)), sem((PARTS, 4)), sem((PARTS,)), sem((PARTS,)),
-            sem((4, 2 * PARTS)), sem((4, 2 * PARTS)), sem((4, CHUNKS)), sem((4, CHUNKS)),
-            sem((4, CHUNKS)), sem((4, CHUNKS)), sem((4,)), sem((4,)),
+            sem((4, 2 * PARTS)), sem((4, 2 * PARTS)), sem((4, 2 * CHUNKS)), sem((4, 2 * CHUNKS)),
+            sem((4, 2 * CHUNKS)), sem((4, 2 * CHUNKS)), sem((4,)), sem((4,)),
             sem((SLOTS, 2)), sem((8 * CHUNKS,)),
         ],
         compiler_params=pltpu.CompilerParams(
             collective_id=0, has_side_effects=True, vmem_limit_bytes=62 * 1024 * 1024
         ),
-    )(hidden, dispatch, picks, gate_weights, gate_proj, up_proj, down_proj)
+    )(hidden, expert_ids.T, gate_weights.T, gate_proj, up_proj, down_proj)
 
 
 def solution(mesh):

time: 84.6 us -> 76.7 us (0.907); the launches traced: 84.1 us -> 75.2 us
  Pallas kernels: 76.7 us -> 73.6 us
  other arithmetic: 2.9 us -> 0 us
  local copies, waits for them, and re-layouts: 4.5 us -> 1.62 us
    pallas_call x1, Pallas kernels: 76.7 us -> 73.6 us  [on_device_paired(): pl.pallas_call(layer_kernel, out_shape=jax.ShapeDtypeStruct((tokens, widt...]
    unnamed x3 -> x1, local copies, waits for them, and re-layouts: 3.81 us -> 1.62 us
    convert_element_type x3 -> x0, other arithmetic: 1.44 us -> none  [the longest x1 0.78 us: on_device_paired(): picks = (slot_of.T.reshape(-1, 1) == slot_range).astype(jnp.bfloat16)]
where the time goes in v1:
time: 76.7 us; the launch traced here: 75.2 us
  Pallas kernels  73.6 us (96%)
  local copies, waits for them, and re-layouts  1.62 us (2%)
    pallas_call x1, Pallas kernels, on_device_paired(): pl.pallas_call(layer_kernel, out_shape=jax.ShapeDtypeStruct((tokens, widt...  73.6 us
    unnamed x1, local copies, waits for them, and re-layouts  1.62 us

profile of v1, /device:TPU:0, one launch (start us, length us, event | category | flops | bytes accessed | tf_op | source)
XLA Modules:
  0.0 75.2 jit_solution(6817427116929120478)
XLA Ops:
  0.0 73.6 %shard_map.64 = bf16[128,768]{1,0:T(8,128)(2,1)} custom-call(bf16[128,768]{1,0:T(8,128)(2,1)} %hidden_ref.1, s32[2,128]{1,0:T(2,128)} %bitcast.2, f32[2,128]{1,0:T(2,128)} %bitcast.3, bf16[1,6144,2048]{2,1,0:T(8,128)(2,1)} %gate_ref.1, bf16[1,6144,2048]{2,1,0:T(8,128)(2,1)} %up_ref.1, bf16[1,768,16384]{2,1,0:T(8,128)(2,1)} %down_ref.1), custom_call_target="tpu_custom_call" | custom-call | tf_op jit(solution)/shard_map/pallas_call | solution.py:427
  73.6 1.6 %copy.8 = bf16[128,768]{1,0:T(8,128)(2,1)} copy(bf16[128,768]{1,0:T(8,128)(2,1)} %shard_map.64) | data formatting | bytes 393216
